TPU v7x, 256 devices: a whole 4x4x8 slice. The times are simulated.
256 devices in a mesh: rep: 4 (over z_lo, core), shard: 64 (over z_hi, y, x).
Axes of the slice: x: 4, y: 4, z: 8 (z_hi: 4, z_lo: 2; z = z_hi * 2 + z_lo), core: 2. Of those that a mesh axis runs over, the one named last changes fastest.
Arguments:
- conv_input: bfloat16 [256, 256, 6144], P(('rep', 'shard')), may hold values from -24 to 24
- cotangent: bfloat16 [256, 256, 6144], P(('rep', 'shard')), may hold values from -24 to 24
- kernel: bfloat16 [31, 6144], P(None, 'shard'), may hold values from -1 to 1
- conv_bias: bfloat16 [6144], P('shard'), may hold values from -3 to 3
- ln_gain: bfloat16 [6144], P('shard'), may hold values from 0.25 to 1.75
- ln_bias: bfloat16 [6144], P('shard'), may hold values from -3 to 3
Outputs:
- activated: bfloat16 [256, 256, 6144], P(('rep', 'shard'))
- grad_input: bfloat16 [256, 256, 6144], P(('rep', 'shard'))
- grad_kernel: float32 [31, 6144], P(None, 'shard')
- grad_conv_bias: float32 [6144], P('shard')
- grad_gain: float32 [6144], P('shard')
- grad_ln_bias: float32 [6144], P('shard')
All inputs are finite; a program needn't handle non-finite values.
Results may differ from a plain program's by a relative error of at most 0.0012.
Values may be sent and summed in bfloat16 or wider, within the bound.
No kernel may reach another device: no remote copies, remote signals or barrier semaphores. Data moves between devices by JAX's collectives and lax.ppermute only.
A program may use at most 128 MiB of HBM per device.

v0:
```python
import math
import jax
import jax.numpy as jnp
from jax import lax
from jax.sharding import PartitionSpec as P


def forward_part(frames_in, params):
    taps = params.shape[0] - 3
    half_width = (taps - 1) // 2
    length = frames_in.shape[0]
    padded = jnp.pad(frames_in, ((half_width, half_width), (0, 0)))
    conv_out = params[taps].astype(jnp.float32)[None, :] + params[0].astype(jnp.float32) * padded[
        0:length
    ].astype(jnp.float32)
    for lag_index in range(1, taps):
        conv_out = conv_out + params[lag_index].astype(jnp.float32) * padded[
            lag_index : lag_index + length
        ].astype(jnp.float32)
    row_mean = jnp.mean(conv_out, axis=-1, keepdims=True)
    centered = conv_out - row_mean
    inverse = lax.rsqrt(jnp.mean(centered * centered, axis=-1, keepdims=True) + 1e-05)
    normed = centered * inverse
    affine = params[taps + 1].astype(jnp.float32) * normed + params[taps + 2].astype(jnp.float32)
    squash = jax.nn.sigmoid(affine)
    activated = (affine * squash).astype(jnp.bfloat16)
    return (activated, normed, inverse, affine, squash)


def backward_part(frames_in, upstream, params, normed, inverse, affine, squash):
    taps = params.shape[0] - 3
    half_width = (taps - 1) // 2
    length = frames_in.shape[0]
    grad_affine = upstream.astype(jnp.float32) * squash * (1.0 + affine * (1.0 - squash))
    grad_normed = grad_affine * params[taps + 1].astype(jnp.float32)
    grad_conv = inverse * (
        grad_normed
        - jnp.mean(grad_normed, axis=-1, keepdims=True)
        - normed * jnp.mean(grad_normed * normed, axis=-1, keepdims=True)
    )
    padded_in = jnp.pad(frames_in, ((half_width, half_width), (0, 0)))
    kernel_rows = [
        jnp.sum(grad_conv * padded_in[lag_index : lag_index + length].astype(jnp.float32), axis=0)
        for lag_index in range(taps)
    ]
    padded_grad = jnp.pad(grad_conv, ((half_width, half_width), (0, 0)))
    back_start = 2 * half_width
    grad_input = params[0].astype(jnp.float32) * padded_grad[back_start : back_start + length]
    for lag_index in range(1, taps):
        first = back_start - lag_index
        grad_input = (
            grad_input + params[lag_index].astype(jnp.float32) * padded_grad[first : first + length]
        )
    terms = jnp.concatenate(
        [
            jnp.stack(kernel_rows, 0),
            jnp.sum(grad_conv, axis=0)[None],
            jnp.sum(grad_affine * normed, axis=0)[None],
            jnp.sum(grad_affine, axis=0)[None],
        ],
        0,
    )
    return (grad_input.astype(jnp.bfloat16), terms)


def per_device(conv_input, cotangent, kernel, conv_bias, ln_gain, ln_bias):
    taps = kernel.shape[0]
    packed = jnp.concatenate([kernel, conv_bias[None], ln_gain[None], ln_bias[None]], 0)
    gathered = lax.all_gather(packed, "shard", axis=1, tiled=True)
    activated, normed, inverse, affine, squash = jax.vmap(forward_part, in_axes=(0, None))(
        conv_input, gathered
    )
    again = lax.all_gather(packed, "shard", axis=1, tiled=True)
    grad_input, terms = jax.vmap(backward_part, in_axes=(0, 0, None, 0, 0, 0, 0))(
        conv_input, cotangent, again, normed, inverse, affine, squash
    )
    terms = jnp.sum(terms, axis=0)
    replicas = lax.axis_size("rep")
    groups = lax.axis_size("shard")
    share_sum = lax.psum_scatter(terms, "shard", scatter_dimension=1, tiled=True)
    summed = lax.psum(share_sum, "rep")
    factor = 1.0 / math.sqrt(conv_input.shape[0] * conv_input.shape[1] * replicas * groups)
    grads = summed * factor
    return (activated, grad_input, grads[:taps], grads[taps], grads[taps + 1], grads[taps + 2])


def solution(mesh):
    in_specs = (
        P(("rep", "shard"), None, None),
        P(("rep", "shard"), None, None),
        P(None, "shard"),
        P("shard"),
        P("shard"),
        P("shard"),
    )
    out_specs = (
        P(("rep", "shard"), None, None),
        P(("rep", "shard"), None, None),
        P(None, "shard"),
        P("shard"),
        P("shard"),
        P("shard"),
    )
    return jax.shard_map(
        per_device, mesh=mesh, in_specs=in_specs, out_specs=out_specs, check_vma=False
    )
```

profile of v0, /device:TPU:1, one launch (start us, length us, event | category | flops | bytes accessed | tf_op | source)
XLA Modules:
  0.0 571.3 jit_solution(10006896554556620029)
XLA Ops:
  7.2 0.0 copy-start.2
  7.2 0.0 reduce-scatter.4.cloned.1.call-start
  7.2 0.9 maximum_bitcast_fusion.1
  8.1 171.1 %all-gather = bf16[64,96,34]{1,2,0:T(8,128)(2,1)S(1)} all-gather(bf16[1,96,34]{1,2,0:T(8,128)(2,1)S(1)} %maximum_bitcast_fusion.1), channel_id=1, replica_groups=mesh['rep'=4,'shard'=64] {'shard'}, dimensions={0}, use_global_device_ids=true | all-gather | bytes 424320 | tf_op jit(solution)/shard_map/all_gather | solution.py:69
  179.2 0.9 copy.13
  180.1 2.6 reshape.462
  182.8 2.5 slice_convert_fusion.32
  185.3 3.1 slice_convert_fusion.33
  188.4 0.0 copy-done.2
  188.4 37.1 %fusion.123 = (f32[256]{0:T(256)S(1)}, f32[1,256,6144]{2,1,0:T(8,128)}) fusion(f32[6144]{0:T(1024)S(1)} %bitcast.121, f32[6144]{0:T(1024)S(1)} %bitcast.123, f32[6144]{0:T(1024)} %bitcast.125, f32[6144]{0:T(1024)} %bitcast.127, f32[6144]{0:T(1024)} %bitcast.129, f32[6144]{0:T(1024)} %bitcast.131, f32[6144]{0:T(1024)} %bitcast.133, f32[6144]{0:T(1024)} %bitcast.135, ...), kind=kLoop, calls=%fused_computation.269 | loop fusion | flops 147848960 | bytes 10224640 | tf_op jit(solution)/shard_map/vmap()/reduce_sum | solution.py:20
  225.5 0.0 copy-start.1
  225.5 3.7 multiply_reduce_fusion.2
  229.3 0.9 copy-done.1
  230.1 9.2 %multiply_reduce_fusion = (f32[6144]{0:T(1024)}, f32[256]{0:T(256)S(1)}, f32[256]{0:T(256)S(1)}, f32[6144]{0:T(1024)}, f32[1,256,6144]{2,1,0:T(8,128)S(1)}, /*index=5*/bf16[1,256,6144]{2,1,0:T(8,128)(2,1)}) fusion(f32[1,256,6144]{2,1,0:T(8,128)S(1)} %copy-done.1, f32[256]{0:T(256)S(1)} %add_rsqrt_fusion, f32[256]{0:T(256)S(1)} %broadcast_multiply_fusion.3, ...), kind=kLoop, calls=%fused_computation.215 | loop fusion | flops 34590208 | bytes 18976768 | tf_op jit(solution)/shard_map/vmap()/reduce_sum | solution.py:58
  239.4 0.0 copy-done.18
  239.4 11.6 %fusion.122 = (f32[6144]{0:T(1024)}, f32[6144]{0:T(1024)}, f32[6144]{0:T(1024)}, f32[6144]{0:T(1024)}, f32[6144]{0:T(1024)}, /*index=5*/f32[6144]{0:T(1024)}, f3...) fusion(bf16[1,256,6144]{2,1,0:T(8,128)(2,1)S(1)} %copy-done.2, f32[256]{0:T(256)S(1)} %get-tuple-element.84, ...), kind=kLoop, calls=%fused_computation.214 | loop fusion | flops 53422080 | bytes 22269952 | tf_op jit(solution)/shard_map/vmap()/reduce_sum | solution.py:43
  251.0 4.3 fusion.89
  255.3 8.5 %fusion.98 = (f32[6144]{0:T(1024)}, f32[6144]{0:T(1024)}, f32[6144]{0:T(1024)}, f32[6144]{0:T(1024)}, f32[6144]{0:T(1024)}, /*index=5*/f32[6144]{0:T(1024)}, f32[6144]{0:T(1024)}, f32[6144]{0:T(1024)}, f32[6144]{0:T(1024)}) fusion(f32[1,256,6144]{2,1,0:T(8,128)S(1)} %get-tuple-element.42, bf16[1,256,6144]{2,1,0:T(8,128)(2,1)S(1)} %copy-done.2), kind=kLoop, calls=%fused_computation.190 | loop fusion | flops 42412032 | bytes 9658368 | tf_op jit(solution)/shard_map/vmap()/reduce_sum | solution.py:43
  263.8 0.0 copy-done
  263.8 8.9 %fusion.107 = (f32[6144]{0:T(1024)}, f32[6144]{0:T(1024)}, f32[6144]{0:T(1024)}, f32[6144]{0:T(1024)}, f32[6144]{0:T(1024)}, /*index=5*/f32[6144]{0:T(1024)}, f3...) fusion(f32[1,256,6144]{2,1,0:T(8,128)S(1)} %get-tuple-element.42, bf16[1,256,6144]{2,1,0:T(8,128)(2,1)S(1)} %copy-done.2), kind=kLoop, calls=%fused_computation.199 | loop fusion | flops 43978752 | bytes 9682944 | tf_op jit(solution)/shard_map/vmap()/reduce_sum | solution.py:43
  272.8 0.0 copy-start.8
  272.8 0.0 copy-start.9
  272.8 0.0 copy-start.10
  272.8 0.0 copy-start.11
  272.8 0.0 copy-start.12
  272.8 0.0 copy-start.13
  272.8 0.0 copy-start.14
  272.8 0.0 copy-start.15
  272.8 0.0 copy-start.16
  272.8 0.0 copy-start.17
  272.9 4.5 stack.127
  277.4 0.9 maximum_bitcast_fusion
  278.3 2.3 copy.14
  280.6 0.0 reduce-scatter.4.cloned.1.call-update
  280.6 0.0 copy-done.3
  280.7 0.0 copy-done.4
  280.7 0.0 copy-done.5
  280.7 0.0 copy-done.6
  280.7 0.0 copy-done.7
  280.7 0.0 copy-done.8
  280.7 0.0 copy-done.9
  280.7 0.0 copy-done.10
  280.8 88.0 %fusion.54 = bf16[1,256,6144]{2,1,0:T(8,128)(2,1)} fusion(f32[1,256,6144]{2,1,0:T(8,128)} %copy-done, f32[6144]{0:T(1024)S(1)} %bitcast.122, f32[6144]{0:T(1024)S(1)} %bitcast.124, f32[6144]{0:T(1024)S(1)} %bitcast.126, f32[6144]{0:T(1024)S(1)} %bitcast.128, f32[6144]{0:T(1024)S(1)} %bitcast.130, f32[6144]{0:T(1024)S(1)} %bitcast.132, ...), kind=kLoop, calls=%fused_computation.146 | loop fusion | flops 97517568 | bytes 10199040 | tf_op jit(solution)/shard_map/vmap()/convert_element_type | solution.py:63
  368.8 181.7 %reduce-scatter.4.cloned.1.call-done = f32[96,34]{1,0:T(8,128)} async-done(((f32[6144,34]{1,0:T(8,128)}), f32[96,34]{1,0:T(8,128)}) %reduce-scatter.4.cloned.1.call-update) | async-done | bytes 13072
  550.6 0.9 copy.15
  551.4 11.9 %psum.7 = f32[34,96]{1,0:T(8,128)S(1)} all-reduce(f32[34,96]{1,0:T(8,128)S(1)} %copy.15), channel_id=1, replica_groups=mesh['rep'=4,'shard'=64] {'rep'}, use_global_device_ids=true, to_apply=%region_39.40 | all-reduce | flops 3264 | bytes 26112 | tf_op jit(solution)/shard_map/psum | solution.py:81
  563.3 0.5 slice_bitcast_fusion
  563.9 0.6 slice.491
  (18 shorter events, 0.0 us)
Async XLA Ops:
  7.2 181.2 %copy-start.2 = (bf16[1,256,6144]{2,1,0:T(8,128)(2,1)S(1)}, bf16[1,256,6144]{2,1,0:T(8,128)(2,1)}, u32[]{:S(2)}) copy-start(bf16[1,256,6144]{2,1,0:T(8,128)(2,1)} %param.6) | copy-start | bytes 9437188
  7.2 543.4 %reduce-scatter.4.cloned.1.call-start = ((), (), s32[]{:S(2)}) async-start(), calls=%async_computation.1 | async-start | bytes 3194880
  225.5 4.6 copy-start.1
  230.1 9.2 %copy-start.18 = (f32[1,6144]{1,0:T(1,128)S(1)}, f32[1,6144]{1,0:T(1,128)}, u32[]{:S(2)}) copy-start(f32[1,6144]{1,0:T(1,128)} %get-tuple-element.47) | copy-start | bytes 73732
  251.0 12.8 %copy-start = (f32[1,256,6144]{2,1,0:T(8,128)}, f32[1,256,6144]{2,1,0:T(8,128)S(1)}, u32[]{:S(2)}) copy-start(f32[1,256,6144]{2,1,0:T(8,128)S(1)} %get-tuple-element.42) | copy-start | bytes 18874372
  272.7 7.9 %copy-start.3 = (f32[1,6144]{1,0:T(1,128)S(1)}, f32[1,6144]{1,0:T(1,128)}, u32[]{:S(2)}) copy-start(f32[1,6144]{1,0:T(1,128)} %get-tuple-element.51) | copy-start | bytes 73732
  272.7 7.9 %copy-start.4 = (f32[1,6144]{1,0:T(1,128)S(1)}, f32[1,6144]{1,0:T(1,128)}, u32[]{:S(2)}) copy-start(f32[1,6144]{1,0:T(1,128)} %get-tuple-element.52) | copy-start | bytes 73732
  272.7 7.9 %copy-start.5 = (f32[1,6144]{1,0:T(1,128)S(1)}, f32[1,6144]{1,0:T(1,128)}, u32[]{:S(2)}) copy-start(f32[1,6144]{1,0:T(1,128)} %get-tuple-element.53) | copy-start | bytes 73732
  272.7 7.9 %copy-start.6 = (f32[1,6144]{1,0:T(1,128)S(1)}, f32[1,6144]{1,0:T(1,128)}, u32[]{:S(2)}) copy-start(f32[1,6144]{1,0:T(1,128)} %get-tuple-element.54) | copy-start | bytes 73732
  272.7 7.9 %copy-start.7 = (f32[1,6144]{1,0:T(1,128)S(1)}, f32[1,6144]{1,0:T(1,128)}, u32[]{:S(2)}) copy-start(f32[1,6144]{1,0:T(1,128)} %get-tuple-element.55) | copy-start | bytes 73732
  272.8 7.9 %copy-start.8 = (f32[1,6144]{1,0:T(1,128)S(1)}, f32[1,6144]{1,0:T(1,128)}, u32[]{:S(2)}) copy-start(f32[1,6144]{1,0:T(1,128)} %get-tuple-element.56) | copy-start | bytes 73732
  272.8 7.9 %copy-start.9 = (f32[1,6144]{1,0:T(1,128)S(1)}, f32[1,6144]{1,0:T(1,128)}, u32[]{:S(2)}) copy-start(f32[1,6144]{1,0:T(1,128)} %get-tuple-element.57) | copy-start | bytes 73732
  272.8 7.9 %copy-start.10 = (f32[1,6144]{1,0:T(1,128)S(1)}, f32[1,6144]{1,0:T(1,128)}, u32[]{:S(2)}) copy-start(f32[1,6144]{1,0:T(1,128)} %get-tuple-element.58) | copy-start | bytes 73732
  272.8 7.9 %copy-start.11 = (f32[1,6144]{1,0:T(1,128)S(1)}, f32[1,6144]{1,0:T(1,128)}, u32[]{:S(2)}) copy-start(f32[1,6144]{1,0:T(1,128)} %get-tuple-element.59) | copy-start | bytes 73732
  272.8 7.9 %copy-start.12 = (f32[1,6144]{1,0:T(1,128)S(1)}, f32[1,6144]{1,0:T(1,128)}, u32[]{:S(2)}) copy-start(f32[1,6144]{1,0:T(1,128)} %get-tuple-element.60) | copy-start | bytes 73732
  272.8 7.9 %copy-start.13 = (f32[1,6144]{1,0:T(1,128)S(1)}, f32[1,6144]{1,0:T(1,128)}, u32[]{:S(2)}) copy-start(f32[1,6144]{1,0:T(1,128)} %get-tuple-element.61) | copy-start | bytes 73732
  272.8 7.9 %copy-start.14 = (f32[1,6144]{1,0:T(1,128)S(1)}, f32[1,6144]{1,0:T(1,128)}, u32[]{:S(2)}) copy-start(f32[1,6144]{1,0:T(1,128)} %get-tuple-element.62) | copy-start | bytes 73732
  272.8 7.9 %copy-start.15 = (f32[1,6144]{1,0:T(1,128)S(1)}, f32[1,6144]{1,0:T(1,128)}, u32[]{:S(2)}) copy-start(f32[1,6144]{1,0:T(1,128)} %get-tuple-element.63) | copy-start | bytes 73732
  272.8 7.9 %copy-start.16 = (f32[1,6144]{1,0:T(1,128)S(1)}, f32[1,6144]{1,0:T(1,128)}, u32[]{:S(2)}) copy-start(f32[1,6144]{1,0:T(1,128)} %get-tuple-element.64) | copy-start | bytes 73732
  272.8 7.9 %copy-start.17 = (f32[1,6144]{1,0:T(1,128)S(1)}, f32[1,6144]{1,0:T(1,128)}, u32[]{:S(2)}) copy-start(f32[1,6144]{1,0:T(1,128)} %get-tuple-element.65) | copy-start | bytes 73732
Sparse Core Ops, SparseCore 0:
  280.8 269.7 reduce-scatter.3
where the time goes:
time: 572 us; the launch traced here: 571 us
  blocking collectives  183 us (32%)
  waiting for transfers between devices  182 us (32%)
  other arithmetic  179 us (31%)
  between operations  14.3 us (2%)
  local copies, waits for them, and re-layouts  13.4 us (2%)
    unnamed x2, waiting for transfers between devices  182 us
    all_gather x1, blocking collectives, per_device(): gathered = lax.all_gather(packed, 'shard', axis=1, tiled=True)  171 us
    convert_element_type x1, other arithmetic, backward_part(): return (grad_input.astype(jnp.bfloat16), terms)  88 us
    reduce_sum x1, other arithmetic, forward_part(): row_mean = jnp.mean(conv_out, axis=-1, keepdims=True)  37.1 us
    reduce_sum x4, other arithmetic, backward_part(): jnp.sum(grad_conv * padded_in[lag_index:lag_index + length].astype(jnp.fl...  33.4 us
    psum x1, blocking collectives, per_device(): summed = lax.psum(share_sum, 'rep')  11.9 us
  transfers between devices with their start and end apart: 1, of which 1 were waited for; matrix products, arithmetic and copies ran while one was open for 15% of the time, Pallas kernels for 0%

commit v1 on v0

--- a/solution.py
+++ b/solution.py
@@ -66,7 +66,9 @@
 def per_device(conv_input, cotangent, kernel, conv_bias, ln_gain, ln_bias):
     taps = kernel.shape[0]
     packed = jnp.concatenate([kernel, conv_bias[None], ln_gain[None], ln_bias[None]], 0)
-    gathered = lax.all_gather(packed, "shard", axis=1, tiled=True)
+    gathered = jnp.concatenate(
+        lax.all_to_all(jnp.stack([packed] * lax.axis_size("shard")), "shard", 0, 0), axis=1
+    )
     activated, normed, inverse, affine, squash = jax.vmap(forward_part, in_axes=(0, None))(
         conv_input, gathered
     )

time: 572 us -> 637 us (1.11)
  local copies, waits for them, and re-layouts: 13.4 us -> 48.7 us
  starting transfers between devices: 0.04 us -> 15.4 us
  other arithmetic: 179 us -> 186 us
    convert_element_type x0 -> x34, local copies, waits for them, and re-layouts: none -> 34.6 us  [the longest x30 29.4 us: forward_part(): params[lag_index].astype(jnp.float32)]
    all_to_all x0 -> x1, starting transfers between devices: none -> 15.3 us  [per_device(): lax.all_to_all(jnp.stack([packed] * lax.axis_size('shard')), 'shard', 0, 0)]
  transfers between devices with their start and end apart: 1 -> 2, of which waited for: 1 -> 1; matrix products, arithmetic and copies ran while one was open for 15% -> 15% of each run, Pallas kernels for 0% -> 0%
where the time goes in v1:
time: 637 us; the launch traced here: 634 us
  other arithmetic  186 us (29%)
  blocking collectives  185 us (29%)
  waiting for transfers between devices  185 us (29%)
  local copies, waits for them, and re-layouts  48.7 us (8%)
  starting transfers between devices  15.4 us (2%)
  between operations  14.7 us (2%)
    unnamed x2, waiting for transfers between devices  185 us
    all_gather x1, blocking collectives, per_device(): again = lax.all_gather(packed, 'shard', axis=1, tiled=True)  173 us
    convert_element_type x1, other arithmetic, backward_part(): return (grad_input.astype(jnp.bfloat16), terms)  88.1 us
    reduce_sum x1, other arithmetic, forward_part(): row_mean = jnp.mean(conv_out, axis=-1, keepdims=True)  37.7 us
    reduce_sum x4, other arithmetic, backward_part(): jnp.sum(grad_conv * padded_in[lag_index:lag_index + length].astype(jnp.fl...  32.1 us
    convert_element_type x30, local copies, waits for them, and re-layouts, forward_part(): params[lag_index].astype(jnp.float32)  29.4 us
    all_to_all x1, starting transfers between devices, per_device(): lax.all_to_all(jnp.stack([packed] * lax.axis_size('shard')), 'shard', 0, 0)  15.3 us
  transfers between devices with their start and end apart: 2, of which 1 were waited for; matrix products, arithmetic and copies ran while one was open for 15% of the time, Pallas kernels for 0%

profile of v1, /device:TPU:1, one launch (start us, length us, event | category | flops | bytes accessed | tf_op | source)
XLA Modules:
  0.0 634.2 jit_solution(2301838018589365052)
XLA Ops:
  7.2 0.9 fusion.157
  8.1 0.9 stack.66
  9.0 15.3 %all-to-all-start = ((bf16[64,34,96]{2,1,0:T(8,128)(2,1)}), bf16[64,34,96]{2,1,0:T(8,128)(2,1)}, u32[]{:S(2)}, u32[]{:S(2)}) async-start(bf16[64,34,96]{2,1,0:T(8,128)(2,1)} %stack.66), calls=%async_computation | async-start | bytes 1310720 | tf_op jit(solution)/shard_map/all_to_all | solution.py:70
  24.4 172.7 %all-gather = bf16[64,96,34]{1,2,0:T(8,128)(2,1)S(1)} all-gather(bf16[1,96,34]{1,2,0:T(8,128)(2,1)S(1)} %get-tuple-element.116), channel_id=1, replica_groups=mesh['rep'=4,'shard'=64] {'shard'}, dimensions={0}, use_global_device_ids=true | all-gather | bytes 424320 | tf_op jit(solution)/shard_map/all_gather | solution.py:75
  197.1 0.9 copy.13
  198.0 2.7 reshape.857
  200.7 3.0 slice_convert_fusion.65
  203.7 2.6 slice_convert_fusion.63
  206.3 4.5 fusion.155
  210.8 4.7 fusion.156
  215.5 0.8 reshape.790
  216.4 1.4 reshape.791
  217.8 1.4 reshape.806
  219.2 1.4 reshape.805
  220.7 1.4 reshape.804
  222.1 1.4 reshape.803
  223.6 1.4 reshape.802
  225.0 1.4 reshape.801
  226.4 1.4 reshape.800
  227.9 1.4 reshape.799
  229.3 1.4 reshape.798
  230.7 1.4 reshape.797
  232.2 1.4 reshape.796
  233.6 1.4 reshape.795
  235.1 1.4 reshape.794
  236.5 1.4 reshape.793
  237.9 1.4 reshape.792
  239.4 1.4 reshape.823
  240.8 1.4 reshape.822
  242.3 1.4 reshape.821
  243.7 1.4 reshape.820
  245.1 1.4 reshape.819
  246.6 1.4 reshape.818
  249.5 0.7 reshape.807
  250.1 37.7 %fusion.158 = (f32[256]{0:T(256)S(1)}, f32[1,256,6144]{2,1,0:T(8,128)}) fusion(f32[6144]{0:T(1024)} %reshape.822, f32[6144]{0:T(1024)} %reshape.821, f32[6144]{0:T(1024)} %reshape.820, f32[6144]{0:T(1024)} %reshape.819, f32[6144]{0:T(1024)} %reshape.818, f32[6144]{0:T(1024)} %reshape.817, f32[6144]{0:T(1024)S(1)} %reshape.816, f32[6144]{0:T(1024)S(1)} %reshape.815, ...), kind=kLoop, calls=%fused_computation.336 | loop fusion | flops 147848960 | bytes 10224640 | tf_op jit(solution)/shard_map/vmap()/reduce_sum | solution.py:20
  287.9 3.7 multiply_reduce_fusion.2
  291.6 0.9 copy-done.1
  292.5 8.6 %multiply_reduce_fusion = (f32[6144]{0:T(1024)S(1)}, f32[256]{0:T(256)S(1)}, f32[256]{0:T(256)S(1)}, f32[6144]{0:T(1024)S(1)}, f32[1,256,6144]{2,1,0:T(8,128)S(1)}, /*index=5*/bf16[1,256,6144]{2,1,0:T(8,128)(2,1)}) fusion(f32[1,256,6144]{2,1,0:T(8,128)S(1)} %copy-done.1, f32[256]{0:T(256)S(1)} %add_rsqrt_fusion, f32[256]{0:T(256)S(1)} %broadcast_multiply_fusion.3, ...), kind=kLoop, calls=%fused_computation.215 | loop fusion | flops 34590208 | bytes 19001344 | tf_op jit(solution)/shard_map/vmap()/reduce_sum | solution.py:58
  301.1 11.6 %fusion.122 = (f32[6144]{0:T(1024)}, f32[6144]{0:T(1024)}, f32[6144]{0:T(1024)}, f32[6144]{0:T(1024)}, f32[6144]{0:T(1024)}, /*index=5*/f32[6144]{0:T(1024)}, f3...) fusion(bf16[1,256,6144]{2,1,0:T(8,128)(2,1)S(1)} %copy-done.2, f32[256]{0:T(256)S(1)} %get-tuple-element.118, ...), kind=kLoop, calls=%fused_computation.214 | loop fusion | flops 53422080 | bytes 22269952 | tf_op jit(solution)/shard_map/vmap()/reduce_sum | solution.py:43
  312.7 3.6 fusion.89
  316.4 8.5 %fusion.98 = (f32[6144]{0:T(1024)}, f32[6144]{0:T(1024)}, f32[6144]{0:T(1024)}, f32[6144]{0:T(1024)}, f32[6144]{0:T(1024)}, /*index=5*/f32[6144]{0:T(1024)}, f32[6144]{0:T(1024)}, f32[6144]{0:T(1024)}, f32[6144]{0:T(1024)}) fusion(f32[1,256,6144]{2,1,0:T(8,128)S(1)} %get-tuple-element.76, bf16[1,256,6144]{2,1,0:T(8,128)(2,1)S(1)} %copy-done.2), kind=kLoop, calls=%fused_computation.190 | loop fusion | flops 42412032 | bytes 9658368 | tf_op jit(solution)/shard_map/vmap()/reduce_sum | solution.py:43
  324.9 8.3 %fusion.107 = (f32[6144]{0:T(1024)S(1)}, f32[6144]{0:T(1024)S(1)}, f32[6144]{0:T(1024)S(1)}, f32[6144]{0:T(1024)S(1)}, f32[6144]{0:T(1024)S(1)}, /*index=5*/f32[...) fusion(f32[1,256,6144]{2,1,0:T(8,128)S(1)} %get-tuple-element.76, ...), kind=kLoop, calls=%fused_computation.199 | loop fusion | flops 43978752 | bytes 9682944 | tf_op jit(solution)/shard_map/vmap()/reduce_sum | solution.py:43
  333.5 4.3 stack.195
  338.0 2.3 copy.14
  340.6 88.1 %fusion.54 = bf16[1,256,6144]{2,1,0:T(8,128)(2,1)} fusion(f32[1,256,6144]{2,1,0:T(8,128)} %copy-done, f32[6144]{0:T(1024)S(1)} %bitcast.123, f32[6144]{0:T(1024)S(1)} %bitcast.124, f32[6144]{0:T(1024)S(1)} %bitcast.125, f32[6144]{0:T(1024)S(1)} %bitcast.126, f32[6144]{0:T(1024)S(1)} %bitcast.127, f32[6144]{0:T(1024)S(1)} %bitcast.128, ...), kind=kLoop, calls=%fused_computation.146 | loop fusion | flops 97517568 | bytes 10199040 | tf_op jit(solution)/shard_map/vmap()/convert_element_type | solution.py:63
  428.7 184.8 %reduce-scatter.4.cloned.1.call-done = f32[96,34]{1,0:T(8,128)} async-done(((f32[6144,34]{1,0:T(8,128)}), f32[96,34]{1,0:T(8,128)}) %reduce-scatter.4.cloned.1.call-update) | async-done | bytes 13072
  613.5 0.9 copy.15
  614.3 11.9 %psum.7 = f32[34,96]{1,0:T(8,128)S(1)} all-reduce(f32[34,96]{1,0:T(8,128)S(1)} %copy.15), channel_id=1, replica_groups=mesh['rep'=4,'shard'=64] {'rep'}, use_global_device_ids=true, to_apply=%region_39.40 | all-reduce | flops 3264 | bytes 26112 | tf_op jit(solution)/shard_map/psum | solution.py:83
  (89 shorter events, 2.9 us)
Async XLA Ops:
  7.2 243.0 %copy-start.2 = (bf16[1,256,6144]{2,1,0:T(8,128)(2,1)S(1)}, bf16[1,256,6144]{2,1,0:T(8,128)(2,1)}, u32[]{:S(2)}) copy-start(bf16[1,256,6144]{2,1,0:T(8,128)(2,1)} %param.6) | copy-start | bytes 9437188
  9.0 197.3 %all-to-all-start = ((bf16[64,34,96]{2,1,0:T(8,128)(2,1)}), bf16[64,34,96]{2,1,0:T(8,128)(2,1)}, u32[]{:S(2)}, u32[]{:S(2)}) async-start(bf16[64,34,96]{2,1,0:T(8,128)(2,1)} %stack.66), calls=%async_computation | async-start | bytes 1310720 | tf_op jit(solution)/shard_map/all_to_all | solution.py:70
  24.4 589.1 %reduce-scatter.4.cloned.1.call-start = ((), (), s32[]{:S(2)}) async-start(), calls=%async_computation.2 | async-start | bytes 3194880
  250.1 41.5 %copy-start.3 = (f32[6144]{0:T(1024)S(1)}, f32[6144]{0:T(1024)}, u32[]{:S(2)}) copy-start(f32[6144]{0:T(1024)} %reshape.823) | copy-start | bytes 73732
  287.9 4.6 copy-start.1
  312.7 12.2 %copy-start = (f32[1,256,6144]{2,1,0:T(8,128)}, f32[1,256,6144]{2,1,0:T(8,128)S(1)}, u32[]{:S(2)}) copy-start(f32[1,256,6144]{2,1,0:T(8,128)S(1)} %get-tuple-element.76) | copy-start | bytes 18874372
  333.2 7.1 %copy-start.4 = (f32[1,6144]{1,0:T(1,128)S(1)}, f32[1,6144]{1,0:T(1,128)}, u32[]{:S(2)}) copy-start(f32[1,6144]{1,0:T(1,128)} %get-tuple-element.100) | copy-start | bytes 73732
  333.2 7.1 %copy-start.5 = (f32[1,6144]{1,0:T(1,128)S(1)}, f32[1,6144]{1,0:T(1,128)}, u32[]{:S(2)}) copy-start(f32[1,6144]{1,0:T(1,128)} %get-tuple-element.101) | copy-start | bytes 73732
  333.2 7.1 %copy-start.6 = (f32[1,6144]{1,0:T(1,128)S(1)}, f32[1,6144]{1,0:T(1,128)}, u32[]{:S(2)}) copy-start(f32[1,6144]{1,0:T(1,128)} %get-tuple-element.102) | copy-start | bytes 73732
  333.3 7.1 %copy-start.7 = (f32[1,6144]{1,0:T(1,128)S(1)}, f32[1,6144]{1,0:T(1,128)}, u32[]{:S(2)}) copy-start(f32[1,6144]{1,0:T(1,128)} %get-tuple-element.103) | copy-start | bytes 73732
  333.3 7.1 %copy-start.8 = (f32[1,6144]{1,0:T(1,128)S(1)}, f32[1,6144]{1,0:T(1,128)}, u32[]{:S(2)}) copy-start(f32[1,6144]{1,0:T(1,128)} %get-tuple-element.104) | copy-start | bytes 73732
  333.3 7.1 %copy-start.9 = (f32[1,6144]{1,0:T(1,128)S(1)}, f32[1,6144]{1,0:T(1,128)}, u32[]{:S(2)}) copy-start(f32[1,6144]{1,0:T(1,128)} %get-tuple-element.105) | copy-start | bytes 73732
  333.3 7.1 %copy-start.10 = (f32[1,6144]{1,0:T(1,128)S(1)}, f32[1,6144]{1,0:T(1,128)}, u32[]{:S(2)}) copy-start(f32[1,6144]{1,0:T(1,128)} %get-tuple-element.106) | copy-start | bytes 73732
  333.3 7.1 %copy-start.11 = (f32[1,6144]{1,0:T(1,128)S(1)}, f32[1,6144]{1,0:T(1,128)}, u32[]{:S(2)}) copy-start(f32[1,6144]{1,0:T(1,128)} %get-tuple-element.107) | copy-start | bytes 73732
  333.3 7.1 %copy-start.12 = (f32[1,6144]{1,0:T(1,128)S(1)}, f32[1,6144]{1,0:T(1,128)}, u32[]{:S(2)}) copy-start(f32[1,6144]{1,0:T(1,128)} %get-tuple-element.108) | copy-start | bytes 73732
  333.3 7.1 %copy-start.13 = (f32[1,6144]{1,0:T(1,128)S(1)}, f32[1,6144]{1,0:T(1,128)}, u32[]{:S(2)}) copy-start(f32[1,6144]{1,0:T(1,128)} %get-tuple-element.109) | copy-start | bytes 73732
  333.3 7.1 %copy-start.14 = (f32[1,6144]{1,0:T(1,128)S(1)}, f32[1,6144]{1,0:T(1,128)}, u32[]{:S(2)}) copy-start(f32[1,6144]{1,0:T(1,128)} %get-tuple-element.110) | copy-start | bytes 73732
  333.3 7.1 %copy-start.15 = (f32[1,6144]{1,0:T(1,128)S(1)}, f32[1,6144]{1,0:T(1,128)}, u32[]{:S(2)}) copy-start(f32[1,6144]{1,0:T(1,128)} %get-tuple-element.111) | copy-start | bytes 73732
  333.3 7.1 %copy-start.16 = (f32[1,6144]{1,0:T(1,128)S(1)}, f32[1,6144]{1,0:T(1,128)}, u32[]{:S(2)}) copy-start(f32[1,6144]{1,0:T(1,128)} %get-tuple-element.81) | copy-start | bytes 73732
  333.4 7.1 %copy-start.17 = (f32[1,6144]{1,0:T(1,128)S(1)}, f32[1,6144]{1,0:T(1,128)}, u32[]{:S(2)}) copy-start(f32[1,6144]{1,0:T(1,128)} %get-tuple-element.82) | copy-start | bytes 73732
  333.4 7.1 %copy-start.18 = (f32[1,6144]{1,0:T(1,128)S(1)}, f32[1,6144]{1,0:T(1,128)}, u32[]{:S(2)}) copy-start(f32[1,6144]{1,0:T(1,128)} %get-tuple-element.83) | copy-start | bytes 73732
  333.4 7.1 %copy-start.19 = (f32[1,6144]{1,0:T(1,128)S(1)}, f32[1,6144]{1,0:T(1,128)}, u32[]{:S(2)}) copy-start(f32[1,6144]{1,0:T(1,128)} %get-tuple-element.84) | copy-start | bytes 73732
  333.4 7.1 %copy-start.20 = (f32[1,6144]{1,0:T(1,128)S(1)}, f32[1,6144]{1,0:T(1,128)}, u32[]{:S(2)}) copy-start(f32[1,6144]{1,0:T(1,128)} %get-tuple-element.85) | copy-start | bytes 73732
  333.4 7.1 %copy-start.21 = (f32[1,6144]{1,0:T(1,128)S(1)}, f32[1,6144]{1,0:T(1,128)}, u32[]{:S(2)}) copy-start(f32[1,6144]{1,0:T(1,128)} %get-tuple-element.86) | copy-start | bytes 73732
  333.4 7.1 %copy-start.22 = (f32[1,6144]{1,0:T(1,128)S(1)}, f32[1,6144]{1,0:T(1,128)}, u32[]{:S(2)}) copy-start(f32[1,6144]{1,0:T(1,128)} %get-tuple-element.87) | copy-start | bytes 73732
  333.4 7.1 %copy-start.23 = (f32[1,6144]{1,0:T(1,128)S(1)}, f32[1,6144]{1,0:T(1,128)}, u32[]{:S(2)}) copy-start(f32[1,6144]{1,0:T(1,128)} %get-tuple-element.88) | copy-start | bytes 73732
  333.4 7.1 %copy-start.24 = (f32[1,6144]{1,0:T(1,128)S(1)}, f32[1,6144]{1,0:T(1,128)}, u32[]{:S(2)}) copy-start(f32[1,6144]{1,0:T(1,128)} %get-tuple-element.89) | copy-start | bytes 73732
  333.4 7.1 %copy-start.25 = (f32[1,6144]{1,0:T(1,128)S(1)}, f32[1,6144]{1,0:T(1,128)}, u32[]{:S(2)}) copy-start(f32[1,6144]{1,0:T(1,128)} %get-tuple-element.90) | copy-start | bytes 73732
  333.4 7.1 %copy-start.26 = (f32[1,6144]{1,0:T(1,128)S(1)}, f32[1,6144]{1,0:T(1,128)}, u32[]{:S(2)}) copy-start(f32[1,6144]{1,0:T(1,128)} %get-tuple-element.91) | copy-start | bytes 73732
  333.5 7.1 %copy-start.27 = (f32[1,6144]{1,0:T(1,128)S(1)}, f32[1,6144]{1,0:T(1,128)}, u32[]{:S(2)}) copy-start(f32[1,6144]{1,0:T(1,128)} %get-tuple-element.92) | copy-start | bytes 73732
  333.5 7.1 %copy-start.28 = (f32[1,6144]{1,0:T(1,128)S(1)}, f32[1,6144]{1,0:T(1,128)}, u32[]{:S(2)}) copy-start(f32[1,6144]{1,0:T(1,128)} %get-tuple-element.93) | copy-start | bytes 73732
  333.5 7.1 %copy-start.29 = (f32[1,6144]{1,0:T(1,128)S(1)}, f32[1,6144]{1,0:T(1,128)}, u32[]{:S(2)}) copy-start(f32[1,6144]{1,0:T(1,128)} %get-tuple-element.94) | copy-start | bytes 73732
  333.5 7.1 %copy-start.30 = (f32[1,6144]{1,0:T(1,128)S(1)}, f32[1,6144]{1,0:T(1,128)}, u32[]{:S(2)}) copy-start(f32[1,6144]{1,0:T(1,128)} %get-tuple-element.95) | copy-start | bytes 73732
  333.5 7.1 %copy-start.31 = (f32[1,6144]{1,0:T(1,128)S(1)}, f32[1,6144]{1,0:T(1,128)}, u32[]{:S(2)}) copy-start(f32[1,6144]{1,0:T(1,128)} %get-tuple-element.96) | copy-start | bytes 73732
  333.5 7.1 %copy-start.32 = (f32[1,6144]{1,0:T(1,128)S(1)}, f32[1,6144]{1,0:T(1,128)}, u32[]{:S(2)}) copy-start(f32[1,6144]{1,0:T(1,128)} %get-tuple-element.97) | copy-start | bytes 73732
  333.5 7.1 %copy-start.33 = (f32[1,6144]{1,0:T(1,128)S(1)}, f32[1,6144]{1,0:T(1,128)}, u32[]{:S(2)}) copy-start(f32[1,6144]{1,0:T(1,128)} %get-tuple-element.98) | copy-start | bytes 73732
  333.5 7.1 %copy-start.34 = (f32[1,6144]{1,0:T(1,128)S(1)}, f32[1,6144]{1,0:T(1,128)}, u32[]{:S(2)}) copy-start(f32[1,6144]{1,0:T(1,128)} %get-tuple-element.99) | copy-start | bytes 73732
Sparse Core Ops, SparseCore 0:
  340.5 272.9 reduce-scatter.3
